TPU v7x, 32 devices: a whole 2x2x4 slice. The times are simulated.
32 devices in a mesh: dp: 4 (over z), row: 4 (over y, x), col: 2 (over core).
Axes of the slice: x: 2, y: 2, z: 4, core: 2. Of those that a mesh axis runs over, the one named last changes fastest.
Arguments:
- grad_parts: bfloat16 [4, 1, 4, 512, 10240], P('dp', None, 'row', None, 'col'), may hold values from -6 to 6
- params: float32 [1, 4, 512, 10240], P(None, 'row', 'dp', 'col'), may hold values from -6 to 6
- row_second: float32 [1, 4, 512], P(None, 'row'), may hold values from 0.1 to 90
- col_second: float32 [1, 10240], P(None, 'col'), may hold values from 0.02 to 100
Outputs:
- new_params: float32 [1, 4, 512, 10240], P(None, 'row', 'dp', 'col')
- new_row: float32 [1, 4, 512], P(None, 'row', 'dp')
- new_col: float32 [1, 10240], P(None, 'col')
All inputs are finite; a program needn't handle non-finite values.
Results may differ from a plain program's by a relative error of at most 0.0003.
Values sent between devices are 32-bit elements; how exact they have to be, the bound alone decides.
No kernel may reach another device: no remote copies, remote signals or barrier semaphores. Data moves between devices by JAX's collectives and lax.ppermute only.
A program may use at most 64 MiB of HBM per device.

v0:
```python
import jax
import jax.numpy as jnp
from jax import lax
from jax.sharding import PartitionSpec as P

beta_two = 1.0 - 8.0 ** (-0.8)
step_rate = 0.5
tiny_add = 1e-30


def shards(grad_parts, params, row_second, col_second):
    owned_rows = params.shape[2]
    local_cols = params.shape[3]
    slab_rows = row_second.shape[2]
    hidden_width = local_cols * lax.axis_size("col")
    matrix_rows = slab_rows * lax.axis_size("row")
    first_row = lax.axis_index("dp") * owned_rows
    old_owned = lax.dynamic_slice_in_dim(row_second, first_row, owned_rows, 2)
    grad_local = grad_parts[0].astype(jnp.float32)
    gradient = lax.psum_scatter(grad_local, "dp", scatter_dimension=2, tiled=True)
    squares = gradient * gradient + tiny_add
    row_part = jnp.sum(squares, axis=3)
    col_part = jnp.sum(squares, axis=(1, 2))
    row_sum = lax.psum(row_part, "col")
    col_sum = lax.psum(col_part, ("dp", "row"))
    new_row = beta_two * old_owned + (1.0 - beta_two) * (row_sum / hidden_width)
    new_col = beta_two * col_second + (1.0 - beta_two) * (col_sum / matrix_rows)
    row_total = lax.psum(jnp.sum(new_row, axis=(1, 2)), ("dp", "row"))
    row_mean = row_total / matrix_rows
    denominator = new_row[:, :, :, None] * new_col[:, None, None, :] / row_mean[:, None, None, None]
    update = gradient * lax.rsqrt(denominator)
    update_total = lax.psum(jnp.sum(update * update, axis=(1, 2, 3)), ("dp", "row", "col"))
    clip_ratio = jnp.sqrt(update_total / (matrix_rows * hidden_width))
    new_params = params - step_rate * update / jnp.maximum(1.0, clip_ratio)[:, None, None, None]
    return (new_params, new_row, new_col)


def solution(mesh):
    return jax.shard_map(
        shards,
        mesh=mesh,
        in_specs=(
            P("dp", None, "row", None, "col"),
            P(None, "row", "dp", "col"),
            P(None, "row", None),
            P(None, "col"),
        ),
        out_specs=(P(None, "row", "dp", "col"), P(None, "row", "dp"), P(None, "col")),
        check_vma=False,
    )
```

profile of v0, /device:TPU:12, one launch (start us, length us, event | category | flops | bytes accessed | tf_op | source)
XLA Modules:
  0.0 330.2 jit_solution(5967783589630943489)
XLA Ops:
  7.2 0.0 reduce-scatter.2.cloned.1.call-start
  7.2 7.8 %bitcast_convert_fusion = f32[1,1,512,5120]{3,2,1,0:T(8,128)} fusion(bf16[1,1,1,512,5120]{4,3,2,1,0:T(8,128)(2,1)} %param.4), kind=kLoop, calls=%fused_computation | loop fusion | flops 2621440 | bytes 15728640 | tf_op jit(solution)/shard_map/convert_element_type | solution.py:19
  15.0 0.0 reduce-scatter.2.cloned.1.call-update
  15.1 0.0 copy-start.2
  15.1 179.2 %reduce-scatter.2.cloned.1.call-done = f32[1,1,128,5120]{3,2,1,0:T(8,128)} async-done(((f32[1,1,512,5120]{3,2,1,0:T(8,128)}), f32[1,1,128,5120]{3,2,1,0:T(8,128)}) %reduce-scatter.2.cloned.1.call-update) | async-done | bytes 2621456 | tf_op jit(solution)/shard_map/reduce_scatter | solution.py:20
  194.3 0.0 copy-start
  194.3 2.3 fusion
  196.7 2.5 psum.28
  199.1 1.3 fusion.2
  200.4 0.0 copy-start.3
  200.4 66.9 %all-reduce = (f32[1]{0:T(128)}, f32[1,5120]{1,0:T(1,128)S(1)}) all-reduce(f32[1]{0:T(128)} %bitcast.5, f32[1,5120]{1,0:T(1,128)S(1)} %bitcast.13), channel_id=1, replica_groups=mesh['dp'=4,'row'=4,'col'=2] {'dp','row'}, use_global_device_ids=true, to_apply=%region_6.0 | all-reduce | flops 5121 | bytes 40968 | tf_op jit(solution)/shard_map/psum | solution.py:28
  267.9 0.0 copy-done.2
  268.0 0.0 copy-start.1
  268.0 0.0 copy-done
  268.0 1.4 multiply_reduce_fusion
  269.4 49.3 %psum.31 = f32[1]{0:T(128)} all-reduce(f32[1]{0:T(128)} %bitcast.7), channel_id=1, replica_groups=mesh['dp'=4,'row'=4,'col'=2] {'dp','row','col'}, use_global_device_ids=true, to_apply=%region_8.0 | all-reduce | flops 1 | bytes 8 | tf_op jit(solution)/shard_map/psum | solution.py:32
  319.4 3.9 %divide_subtract_fusion = f32[1,1,128,5120]{3,2,1,0:T(8,128)} fusion(f32[1,1,128,5120]{3,2,1,0:T(8,128)} %param.5, f32[]{:T(128)} %bitcast.8, f32[1,1,128,5120]{3,2,1,0:T(8,128)S(1)} %copy-done, f32[]{:T(128)} %bitcast.6, f32[5120]{0:T(1024)S(1)} %bitcast.12, f32[128]{0:T(128)S(1)} %bitcast.15), kind=kLoop, calls=%fused_computation.1 | loop fusion | flops 3932160 | bytes 7885320 | tf_op jit(solution)/shard_map/sub | solution.py:34
  323.3 0.0 copy-done.3
  323.3 0.0 copy-done.1
  (1 shorter events, 0.0 us)
Async XLA Ops:
  7.2 187.2 %reduce-scatter.2.cloned.1.call-start = ((), (), s32[]{:S(2)}) async-start(), calls=%async_computation.1 | async-start | bytes 13107200 | tf_op jit(solution)/shard_map/reduce_scatter | solution.py:20
  15.1 252.8 %copy-start.2 = (f32[1,5120]{1,0:T(1,128)S(1)}, f32[1,5120]{1,0:T(1,128)}, u32[]{:S(2)}) copy-start(f32[1,5120]{1,0:T(1,128)} %param.7) | copy-start | bytes 61444
  194.3 73.6 %copy-start = (f32[1,1,128,5120]{3,2,1,0:T(8,128)S(1)}, f32[1,1,128,5120]{3,2,1,0:T(8,128)}, u32[]{:S(2)}) copy-start(f32[1,1,128,5120]{3,2,1,0:T(8,128)} %reduce-scatter.2.cloned.1.call-done) | copy-start | bytes 7864324
  200.4 122.9 %copy-start.3 = (f32[1,1,128]{2,1,0:T(1,128)}, f32[1,1,128]{2,1,0:T(1,128)S(1)}, u32[]{:S(2)}) copy-start(f32[1,1,128]{2,1,0:T(1,128)S(1)} %get-tuple-element.8) | copy-start | bytes 1540
  268.0 55.4 %copy-start.1 = (f32[1,5120]{1,0:T(1,128)}, f32[1,5120]{1,0:T(1,128)S(1)}, u32[]{:S(2)}) copy-start(f32[1,5120]{1,0:T(1,128)S(1)} %multiply_add_fusion.1) | copy-start | bytes 61444
Sparse Core Ops, SparseCore 0:
  15.2 179.0 reduce-scatter.1
where the time goes:
time: 331 us; the launch traced here: 330 us
  waiting for transfers between devices  179 us (54%)
  blocking collectives  119 us (36%)
  other arithmetic  16.8 us (5%)
  between operations  15.4 us (5%)
    reduce_scatter x1, waiting for transfers between devices, shards(): lax.psum_scatter(grad_local, 'dp', scatter_dimension=2, tiled=True)  179 us
    psum x1, blocking collectives, shards(): row_total = lax.psum(jnp.sum(new_row, axis=(1, 2)), ('dp', 'row'))  66.9 us
    psum x1, blocking collectives, shards(): lax.psum(jnp.sum(update * update, axis=(1, 2, 3)), ('dp', 'row', 'col'))  49.3 us
    convert_element_type x1, other arithmetic, shards(): grad_local = grad_parts[0].astype(jnp.float32)  7.83 us
  transfers between devices with their start and end apart: 1, of which 1 were waited for; matrix products, arithmetic and copies ran while one was open for 0% of the time, Pallas kernels for 0%

commit v1 on v0

--- a/solution.py
+++ b/solution.py
@@ -25,7 +25,9 @@
     col_sum = lax.psum(col_part, ("dp", "row"))
     new_row = beta_two * old_owned + (1.0 - beta_two) * (row_sum / hidden_width)
     new_col = beta_two * col_second + (1.0 - beta_two) * (col_sum / matrix_rows)
-    row_total = lax.psum(jnp.sum(new_row, axis=(1, 2)), ("dp", "row"))
+    own = jnp.sum(new_row, axis=(1, 2))
+    terms = lax.all_gather(own, ("dp", "row"), axis=0, tiled=False)
+    row_total = terms.sum(axis=0)
     row_mean = row_total / matrix_rows
     denominator = new_row[:, :, :, None] * new_col[:, None, None, :] / row_mean[:, None, None, None]
     update = gradient * lax.rsqrt(denominator)

time: 331 us -> 333 us (level)
    psum x1 -> x0, blocking collectives: 66.9 us -> none  [shards(): row_total = lax.psum(jnp.sum(new_row, axis=(1, 2)), ('dp', 'row'))]
    unnamed x0 -> x1, blocking collectives: none -> 66.9 us
where the time goes in v1:
time: 333 us; the launch traced here: 332 us
  waiting for transfers between devices  178 us (53%)
  blocking collectives  119 us (36%)
  other arithmetic  17.4 us (5%)
  between operations  15.4 us (5%)
    reduce_scatter x1, waiting for transfers between devices, shards(): lax.psum_scatter(grad_local, 'dp', scatter_dimension=2, tiled=True)  178 us
    unnamed x1, blocking collectives  66.9 us
    psum x1, blocking collectives, shards(): lax.psum(jnp.sum(update * update, axis=(1, 2, 3)), ('dp', 'row', 'col'))  49.3 us
    convert_element_type x1, other arithmetic, shards(): grad_local = grad_parts[0].astype(jnp.float32)  7.83 us
  transfers between devices with their start and end apart: 1, of which 1 were waited for; matrix products, arithmetic and copies ran while one was open for 0% of the time, Pallas kernels for 0%

profile of v1, /device:TPU:12, one launch (start us, length us, event | category | flops | bytes accessed | tf_op | source)
XLA Modules:
  0.0 332.2 jit_solution(5899271284626905070)
XLA Ops:
  7.2 0.0 reduce-scatter.2.cloned.1.call-start
  7.2 7.8 %bitcast_convert_fusion = f32[1,1,512,5120]{3,2,1,0:T(8,128)} fusion(bf16[1,1,1,512,5120]{4,3,2,1,0:T(8,128)(2,1)} %param.4), kind=kLoop, calls=%fused_computation | loop fusion | flops 2621440 | bytes 15728640 | tf_op jit(solution)/shard_map/convert_element_type | solution.py:19
  15.0 0.0 copy-start.4
  15.0 0.0 reduce-scatter.2.cloned.1.call-update
  15.1 0.0 copy-start.2
  15.1 0.6 copy-done.4
  15.7 0.6 dynamic-slice
  16.3 178.1 %reduce-scatter.2.cloned.1.call-done = f32[1,1,128,5120]{3,2,1,0:T(8,128)} async-done(((f32[1,1,512,5120]{3,2,1,0:T(8,128)}), f32[1,1,128,5120]{3,2,1,0:T(8,128)}) %reduce-scatter.2.cloned.1.call-update) | async-done | bytes 2621456 | tf_op jit(solution)/shard_map/reduce_scatter | solution.py:20
  194.3 0.0 copy-start
  194.3 2.3 fusion
  196.7 2.5 psum.21
  199.1 1.3 fusion.2
  200.4 0.0 copy-start.3
  200.4 1.4 dynamic-update-slice
  201.8 66.9 %all-reduce.1 = (f32[16]{0:T(128)S(1)}, f32[1,5120]{1,0:T(1,128)S(1)}) all-reduce(f32[16]{0:T(128)S(1)} %dynamic-update-slice, f32[1,5120]{1,0:T(1,128)S(1)} %bitcast.13), channel_id=1, replica_groups=mesh['dp'=4,'row'=4,'col'=2] {'dp','row'}, use_global_device_ids=true, to_apply=%add | all-reduce | flops 5136 | bytes 41088
  268.6 0.6 reduce.5
  269.9 0.0 copy-done.2
  270.0 0.0 copy-start.1
  270.0 0.0 copy-done
  270.0 1.4 multiply_reduce_fusion
  271.4 49.3 %psum.23 = f32[1]{0:T(128)} all-reduce(f32[1]{0:T(128)} %bitcast.7), channel_id=1, replica_groups=mesh['dp'=4,'row'=4,'col'=2] {'dp','row','col'}, use_global_device_ids=true, to_apply=%region_8.0 | all-reduce | flops 1 | bytes 8 | tf_op jit(solution)/shard_map/psum | solution.py:34
  321.4 3.9 %divide_subtract_fusion = f32[1,1,128,5120]{3,2,1,0:T(8,128)} fusion(f32[1,1,128,5120]{3,2,1,0:T(8,128)} %param.5, f32[]{:T(128)} %bitcast.8, f32[1,1,128,5120]{3,2,1,0:T(8,128)S(1)} %copy-done, f32[]{:T(128)S(6)} %div.36, f32[5120]{0:T(1024)S(1)} %bitcast.12, f32[128]{0:T(128)S(1)} %bitcast.15), kind=kLoop, calls=%fused_computation.1 | loop fusion | flops 3932160 | bytes 7885320 | tf_op jit(solution)/shard_map/sub | solution.py:36
  325.3 0.0 copy-done.3
  325.3 0.0 copy-done.1
  (2 shorter events, 0.0 us)
Async XLA Ops:
  7.2 187.2 %reduce-scatter.2.cloned.1.call-start = ((), (), s32[]{:S(2)}) async-start(), calls=%async_computation.1 | async-start | bytes 13107200 | tf_op jit(solution)/shard_map/reduce_scatter | solution.py:20
  15.0 0.7 copy-start.4
  15.1 254.8 %copy-start.2 = (f32[1,5120]{1,0:T(1,128)S(1)}, f32[1,5120]{1,0:T(1,128)}, u32[]{:S(2)}) copy-start(f32[1,5120]{1,0:T(1,128)} %param.7) | copy-start | bytes 61444
  194.3 75.6 %copy-start = (f32[1,1,128,5120]{3,2,1,0:T(8,128)S(1)}, f32[1,1,128,5120]{3,2,1,0:T(8,128)}, u32[]{:S(2)}) copy-start(f32[1,1,128,5120]{3,2,1,0:T(8,128)} %reduce-scatter.2.cloned.1.call-done) | copy-start | bytes 7864324
  200.4 124.9 %copy-start.3 = (f32[1,1,128]{2,1,0:T(1,128)}, f32[1,1,128]{2,1,0:T(1,128)S(1)}, u32[]{:S(2)}) copy-start(f32[1,1,128]{2,1,0:T(1,128)S(1)} %get-tuple-element.8) | copy-start | bytes 1540
  270.0 55.4 %copy-start.1 = (f32[1,5120]{1,0:T(1,128)}, f32[1,5120]{1,0:T(1,128)S(1)}, u32[]{:S(2)}) copy-start(f32[1,5120]{1,0:T(1,128)S(1)} %multiply_add_fusion.1) | copy-start | bytes 61444
Sparse Core Ops, SparseCore 0:
  15.2 179.0 reduce-scatter.1

commit v2 on v0

--- a/solution.py
+++ b/solution.py
@@ -25,7 +25,11 @@
     col_sum = lax.psum(col_part, ("dp", "row"))
     new_row = beta_two * old_owned + (1.0 - beta_two) * (row_sum / hidden_width)
     new_col = beta_two * col_second + (1.0 - beta_two) * (col_sum / matrix_rows)
-    row_total = lax.psum(jnp.sum(new_row, axis=(1, 2)), ("dp", "row"))
+
+    def _proceed_ticks(array_in):
+        return jax.lax.psum(jax.lax.psum(array_in, "row"), "dp")
+
+    row_total = _proceed_ticks(jnp.sum(new_row, axis=(1, 2)))
     row_mean = row_total / matrix_rows
     denominator = new_row[:, :, :, None] * new_col[:, None, None, :] / row_mean[:, None, None, None]
     update = gradient * lax.rsqrt(denominator)

time: 331 us -> 348 us (1.051)
  blocking collectives: 119 us -> 136 us
    psum x1 -> x3, blocking collectives: 66.9 us -> 84.6 us  [the longest x1 64.5 us: shards(): col_sum = lax.psum(col_part, ('dp', 'row'))]
where the time goes in v2:
time: 348 us
  waiting for transfers between devices  179 us (51%)
  blocking collectives  136 us (39%)
  other arithmetic  16.8 us (5%)
  between operations  15.4 us (4%)
    reduce_scatter x1, waiting for transfers between devices, shards(): lax.psum_scatter(grad_local, 'dp', scatter_dimension=2, tiled=True)  179 us
    psum x1, blocking collectives, shards(): col_sum = lax.psum(col_part, ('dp', 'row'))  64.5 us
    psum x1, blocking collectives, shards(): lax.psum(jnp.sum(update * update, axis=(1, 2, 3)), ('dp', 'row', 'col'))  49.4 us
    psum x2, blocking collectives, _proceed_ticks(): return jax.lax.psum(jax.lax.psum(array_in, 'row'), 'dp')  20.1 us
    convert_element_type x1, other arithmetic, shards(): grad_local = grad_parts[0].astype(jnp.float32)  7.83 us
  transfers between devices with their start and end apart: 1, of which 1 were waited for; matrix products, arithmetic and copies ran while one was open for 0% of the time, Pallas kernels for 0%

profile of v2, /device:TPU:12, one launch (start us, length us, event | category | flops | bytes accessed | tf_op | source)
XLA Modules:
  0.0 347.9 jit_solution(10339860648267952166)
XLA Ops:
  7.2 0.0 reduce-scatter.2.cloned.1.call-start
  7.2 7.8 %bitcast_convert_fusion = f32[1,1,512,5120]{3,2,1,0:T(8,128)} fusion(bf16[1,1,1,512,5120]{4,3,2,1,0:T(8,128)(2,1)} %param.4), kind=kLoop, calls=%fused_computation | loop fusion | flops 2621440 | bytes 15728640 | tf_op jit(solution)/shard_map/convert_element_type | solution.py:19
  15.0 0.0 reduce-scatter.2.cloned.1.call-update
  15.1 0.0 copy-start.2
  15.1 179.2 %reduce-scatter.2.cloned.1.call-done = f32[1,1,128,5120]{3,2,1,0:T(8,128)} async-done(((f32[1,1,512,5120]{3,2,1,0:T(8,128)}), f32[1,1,128,5120]{3,2,1,0:T(8,128)}) %reduce-scatter.2.cloned.1.call-update) | async-done | bytes 2621456 | tf_op jit(solution)/shard_map/reduce_scatter | solution.py:20
  194.3 0.0 copy-start
  194.3 2.3 fusion
  196.7 2.5 psum.35
  199.1 1.3 fusion.2
  200.4 0.0 copy-start.3
  200.4 9.6 %psum.37 = f32[1]{0:T(128)} all-reduce(f32[1]{0:T(128)} %bitcast.5), channel_id=1, replica_groups=mesh['dp'=4,'row'=4,'col'=2] {'row'}, use_global_device_ids=true, to_apply=%region_6.0 | all-reduce | flops 1 | bytes 8 | tf_op jit(solution)/shard_map/psum | solution.py:30
  209.9 10.6 %psum.38 = f32[1]{0:T(128)} all-reduce(f32[1]{0:T(128)} %psum.37), channel_id=1, replica_groups=mesh['dp'=4,'row'=4,'col'=2] {'dp'}, use_global_device_ids=true, to_apply=%region_7.0 | all-reduce | flops 1 | bytes 8 | tf_op jit(solution)/shard_map/psum | solution.py:30
  220.5 64.5 %psum.36 = f32[1,5120]{1,0:T(1,128)S(1)} all-reduce(f32[1,5120]{1,0:T(1,128)S(1)} %bitcast.13), channel_id=1, replica_groups=mesh['dp'=4,'row'=4,'col'=2] {'dp','row'}, use_global_device_ids=true, to_apply=%region_4.0 | all-reduce | flops 5120 | bytes 40960 | tf_op jit(solution)/shard_map/psum | solution.py:25
  285.7 0.0 copy-done.2
  285.7 0.0 copy-start.1
  285.7 0.0 copy-done
  285.8 1.4 multiply_reduce_fusion
  287.1 49.4 %psum.39 = f32[1]{0:T(128)} all-reduce(f32[1]{0:T(128)} %bitcast.7), channel_id=1, replica_groups=mesh['dp'=4,'row'=4,'col'=2] {'dp','row','col'}, use_global_device_ids=true, to_apply=%region_9.0 | all-reduce | flops 1 | bytes 8 | tf_op jit(solution)/shard_map/psum | solution.py:36
  337.2 3.9 %divide_subtract_fusion = f32[1,1,128,5120]{3,2,1,0:T(8,128)} fusion(f32[1,1,128,5120]{3,2,1,0:T(8,128)} %param.5, f32[]{:T(128)} %bitcast.8, f32[1,1,128,5120]{3,2,1,0:T(8,128)S(1)} %copy-done, f32[]{:T(128)} %bitcast.6, f32[5120]{0:T(1024)S(1)} %bitcast.12, f32[128]{0:T(128)S(1)} %bitcast.15), kind=kLoop, calls=%fused_computation.1 | loop fusion | flops 3932160 | bytes 7885320 | tf_op jit(solution)/shard_map/sub | solution.py:38
  341.1 0.0 copy-done.3
  341.1 0.0 copy-done.1
  (1 shorter events, 0.0 us)
Async XLA Ops:
  7.2 187.2 %reduce-scatter.2.cloned.1.call-start = ((), (), s32[]{:S(2)}) async-start(), calls=%async_computation.1 | async-start | bytes 13107200 | tf_op jit(solution)/shard_map/reduce_scatter | solution.py:20
  15.1 270.6 %copy-start.2 = (f32[1,5120]{1,0:T(1,128)S(1)}, f32[1,5120]{1,0:T(1,128)}, u32[]{:S(2)}) copy-start(f32[1,5120]{1,0:T(1,128)} %param.7) | copy-start | bytes 61444
  194.3 91.4 %copy-start = (f32[1,1,128,5120]{3,2,1,0:T(8,128)S(1)}, f32[1,1,128,5120]{3,2,1,0:T(8,128)}, u32[]{:S(2)}) copy-start(f32[1,1,128,5120]{3,2,1,0:T(8,128)} %reduce-scatter.2.cloned.1.call-done) | copy-start | bytes 7864324
  200.4 140.7 %copy-start.3 = (f32[1,1,128]{2,1,0:T(1,128)}, f32[1,1,128]{2,1,0:T(1,128)S(1)}, u32[]{:S(2)}) copy-start(f32[1,1,128]{2,1,0:T(1,128)S(1)} %get-tuple-element.6) | copy-start | bytes 1540
  285.7 55.4 %copy-start.1 = (f32[1,5120]{1,0:T(1,128)}, f32[1,5120]{1,0:T(1,128)S(1)}, u32[]{:S(2)}) copy-start(f32[1,5120]{1,0:T(1,128)S(1)} %multiply_add_fusion.1) | copy-start | bytes 61444
Sparse Core Ops, SparseCore 0:
  15.2 179.0 reduce-scatter.1
